TPU v7x, 512 devices: a whole 4x4x16 slice. The times are simulated.
512 devices in a mesh: dp: 32 (over y_lo, z), tensor: 16 (over y_hi, x, core).
Axes of the slice: x: 4, y: 4 (y_hi: 2, y_lo: 2; y = y_hi * 2 + y_lo), z: 16, core: 2. Of those that a mesh axis runs over, the one named last changes fastest.
Arguments:
- inputs: bfloat16 [4096, 8192], P('dp', 'tensor'), may hold values from -6 to 6
- grad_context: bfloat16 [4096, 8192], P('dp', 'tensor'), may hold values from -24 to 24
- gain: float32 [8192], replicated, may hold values from 0.1 to 1.9
- w_query: bfloat16 [8192, 8192], P('dp', 'tensor'), may hold values from -0.0625 to 0.0625
- w_keyval: bfloat16 [8192, 1024], P('dp', 'tensor'), may hold values from -0.0625 to 0.0625
Outputs:
- grad_input: bfloat16 [4096, 8192], P('dp', 'tensor')
- grad_gain: float32 [8192], P('tensor')
- grad_w_keyval: bfloat16 [8192, 1024], P('dp', 'tensor')
All inputs are finite; a program needn't handle non-finite values.
Results may differ from a plain program's by a relative error of at most 0.023.
Values may be sent and summed in bfloat16 or wider, within the bound.
A program may use at most 64 MiB of HBM per device.

v0:
```python
import math
import jax
import jax.numpy as jnp
from jax import lax
from jax.sharding import PartitionSpec as P

HD = 128
KV_HEADS = 4
HEADS_DEV = 4


def rope_tables(length, head_size):
    positions = lax.broadcasted_iota(jnp.int32, (length, head_size // 2), 0).astype(jnp.float32)
    index_half = lax.broadcasted_iota(jnp.int32, (length, head_size // 2), 1).astype(jnp.float32)
    frequency = jnp.exp(-(2.0 * index_half / head_size) * math.log(500000.0))
    angles = positions * frequency
    return (jnp.cos(angles), jnp.sin(angles))


def rotate(vectors, cosine_table, sine_table):
    half_size = vectors.shape[-1] // 2
    first_half = vectors[..., :half_size]
    second_half = vectors[..., half_size:]
    return jnp.concatenate(
        [
            first_half * cosine_table - second_half * sine_table,
            first_half * sine_table + second_half * cosine_table,
        ],
        axis=-1,
    )


def unrotate(vectors, cosine_table, sine_table):
    half_size = vectors.shape[-1] // 2
    first_half = vectors[..., :half_size]
    second_half = vectors[..., half_size:]
    return jnp.concatenate(
        [
            first_half * cosine_table + second_half * sine_table,
            second_half * cosine_table - first_half * sine_table,
        ],
        axis=-1,
    )


def on_device(inputs, grad_context, gain, w_query, w_keyval):
    contract_last = (((1,), (1,)), ((), ()))
    contract_first = (((0,), (0,)), ((), ()))
    seq_length = inputs.shape[0]
    local_cols = inputs.shape[1]
    model_width = gain.shape[0]
    head_size = HD
    heads_here = HEADS_DEV
    group_cols = w_keyval.shape[1]
    tensor_count = lax.axis_size("tensor")
    keyval_total = group_cols * tensor_count
    kv_heads = KV_HEADS
    devices_per_group = tensor_count // kv_heads
    score_scale = head_size ** (-0.5)
    tensor_slot = lax.axis_index("tensor")
    gain_local = lax.dynamic_slice_in_dim(gain, tensor_slot * local_cols, local_cols, 0)
    as_float = inputs.astype(jnp.float32)
    row_sum = lax.psum(jnp.sum(as_float * as_float, axis=1, keepdims=True), "tensor")
    inv_rms = lax.rsqrt(row_sum / model_width + 1e-05)
    unit_rows = as_float * inv_rms
    normed = (unit_rows * gain_local).astype(jnp.bfloat16)
    normed_full = lax.all_gather(normed, "tensor", axis=1, tiled=True)
    query_weight, keyweight = (
        lax.all_gather(w_query, "dp", axis=0, tiled=True),
        lax.all_gather(w_keyval, "dp", axis=0, tiled=True),
    )
    query_proj = jnp.dot(normed_full, query_weight, preferred_element_type=jnp.float32).astype(
        jnp.bfloat16
    )
    keyval_part = jnp.dot(normed_full, keyweight, preferred_element_type=jnp.float32).astype(
        jnp.bfloat16
    )
    keyval_full = lax.all_gather(keyval_part, "tensor", axis=1, tiled=True)
    group_slot = tensor_slot // devices_per_group
    key_block = lax.dynamic_slice_in_dim(keyval_full, group_slot * head_size, head_size, 1)
    value_block = lax.dynamic_slice_in_dim(
        keyval_full, (kv_heads + group_slot) * head_size, head_size, 1
    )
    cosine_table, sine_table = rope_tables(seq_length, head_size)
    cos_heads = cosine_table[:, None, :]
    sin_heads = sine_table[:, None, :]
    query_heads = query_proj.astype(jnp.float32).reshape(seq_length, heads_here, head_size)
    q_rot = rotate(query_heads, cos_heads, sin_heads).astype(jnp.bfloat16)
    k_rot = rotate(key_block.astype(jnp.float32), cosine_table, sine_table).astype(jnp.bfloat16)
    scores = (
        jnp.einsum("shd,td->hst", q_rot, k_rot, preferred_element_type=jnp.float32) * score_scale
    )
    causal = lax.broadcasted_iota(jnp.int32, (seq_length, seq_length), 0) >= lax.broadcasted_iota(
        jnp.int32, (seq_length, seq_length), 1
    )
    exponent = jnp.where(causal[None, :, :], jnp.exp(scores), 0.0)
    softmax_probs = exponent / jnp.sum(exponent, axis=2, keepdims=True)
    prob_weights = softmax_probs.astype(jnp.bfloat16)
    context = jnp.einsum(
        "hst,td->shd", prob_weights, value_block, preferred_element_type=jnp.float32
    ).astype(jnp.bfloat16)
    grad_ctx = grad_context.reshape(seq_length, heads_here, head_size)
    grad_probs = jnp.einsum(
        "shd,td->hst", grad_ctx, value_block, preferred_element_type=jnp.float32
    )
    row_delta = jnp.sum(grad_ctx.astype(jnp.float32) * context.astype(jnp.float32), axis=2).T[
        :, :, None
    ]
    grad_scores = (softmax_probs * (grad_probs - row_delta) * score_scale).astype(jnp.bfloat16)
    grad_qrot = jnp.einsum("hst,td->shd", grad_scores, k_rot, preferred_element_type=jnp.float32)
    grad_krot = jnp.einsum("hst,shd->td", grad_scores, q_rot, preferred_element_type=jnp.float32)
    grad_value = jnp.einsum(
        "hst,shd->td", prob_weights, grad_ctx, preferred_element_type=jnp.float32
    )
    grad_query = (
        unrotate(grad_qrot, cos_heads, sin_heads)
        .astype(jnp.bfloat16)
        .reshape(seq_length, heads_here * head_size)
    )
    grad_terms = jnp.zeros((seq_length, keyval_total), jnp.float32)
    grad_terms = lax.dynamic_update_slice_in_dim(
        grad_terms, unrotate(grad_krot, cosine_table, sine_table), group_slot * head_size, 1
    )
    grad_terms = lax.dynamic_update_slice_in_dim(
        grad_terms, grad_value, (kv_heads + group_slot) * head_size, 1
    )
    grad_keyval = lax.psum_scatter(
        grad_terms.astype(jnp.bfloat16), "tensor", scatter_dimension=1, tiled=True
    )
    result = lax.dot_general(
        query_weight, grad_query, contract_last, preferred_element_type=jnp.float32
    )
    grad_normed = (
        lax.psum_scatter(
            (
                result
                + lax.dot_general(
                    keyweight, grad_keyval, contract_last, preferred_element_type=jnp.float32
                )
            ).astype(jnp.bfloat16),
            "tensor",
            scatter_dimension=0,
            tiled=True,
        )
        .astype(jnp.float32)
        .T
    )
    scaled_grad = grad_normed * gain_local
    product_sum = lax.psum(jnp.sum(scaled_grad * unit_rows, axis=1, keepdims=True), "tensor")
    grad_input = (inv_rms * (scaled_grad - unit_rows * (product_sum / model_width))).astype(
        jnp.bfloat16
    )
    grad_gain = lax.psum(jnp.sum(grad_normed * unit_rows, axis=0), "dp")
    keyval_all = lax.all_gather(grad_keyval, "dp", axis=0, tiled=True)
    rows_normed = lax.all_to_all(normed_full, "dp", split_axis=1, concat_axis=0, tiled=True)
    keyval_weight_grad = lax.dot_general(
        rows_normed, keyval_all, contract_first, preferred_element_type=jnp.float32
    )
    return (grad_input, grad_gain, keyval_weight_grad.astype(jnp.bfloat16))


def solution(mesh):
    in_specs = (P("dp", "tensor"), P("dp", "tensor"), P(), P("dp", "tensor"), P("dp", "tensor"))
    out_specs = (P("dp", "tensor"), P("tensor"), P("dp", "tensor"))
    return jax.shard_map(
        on_device, mesh=mesh, in_specs=in_specs, out_specs=out_specs, check_vma=False
    )
```

profile of v0, /device:TPU:16, one launch (start us, length us, event | category | flops | bytes accessed | tf_op | source)
XLA Modules:
  0.0 727.8 jit_solution(10159442751413504950)
XLA Ops:
  7.2 0.0 all-gather.4.cloned.1.call-start
  7.2 1.0 fusion.25
  8.2 35.1 %psum.21 = f32[128,1]{0,1:T(1,128)S(1)} all-reduce(f32[128,1]{0,1:T(1,128)S(1)} %bitcast.94), channel_id=1, replica_groups=mesh['dp'=32,'tensor'=16] {'tensor'}, use_global_device_ids=true, to_apply=%region_1.0 | all-reduce | flops 128 | bytes 1024 | tf_op jit(solution)/shard_map/psum | solution.py:63
  43.4 0.8 dynamic_slice.9
  44.1 1.7 fusion.19
  45.8 0.0 all-gather.4.cloned.1.call-update
  45.8 0.0 all-gather.6.cloned.1.call-start
  45.9 0.7 all-gather.6.cloned.1.call-update
  46.6 0.0 all-gather.8.cloned.1.call-start
  46.6 0.7 all-gather.8.cloned.1.call-update
  47.3 63.7 %all-gather.4.cloned.1.call-done = bf16[128,8192]{1,0:T(8,128)(2,1)} async-done(((bf16[128,512]{1,0:T(8,128)(2,1)}), bf16[128,8192]{1,0:T(8,128)(2,1)}) %all-gather.4.cloned.1.call-update) | async-done | bytes 2097168 | tf_op jit(solution)/shard_map/all_gather | solution.py:67
  111.0 3.2 copy.61
  114.2 0.0 copy-start.4
  114.2 0.0 copy-start
  114.2 14.4 %all-to-all-start = ((bf16[128,32,256]{2,0,1:T(8,128)(2,1)}), bf16[128,32,256]{2,0,1:T(8,128)(2,1)}, u32[]{:S(2)}, u32[]{:S(2)}) async-start(bf16[128,32,256]{2,0,1:T(8,128)(2,1)} %bitcast.87), calls=%async_computation.2 | async-start | bytes 4194304 | tf_op jit(solution)/shard_map/all_to_all | solution.py:155
  128.5 0.0 reduce-scatter.3.cloned.1.call-start
  128.6 0.0 copy-done.4
  128.6 0.1 copy.28
  128.8 156.6 %all-gather.6.cloned.1.call-done = bf16[8192,64]{0,1:T(8,128)(2,1)} async-done(((bf16[256,64]{0,1:T(8,128)(2,1)}), bf16[8192,64]{0,1:T(8,128)(2,1)}) %all-gather.6.cloned.1.call-update) | async-done | bytes 1048592 | tf_op jit(solution)/shard_map/all_gather | solution.py:70
  285.4 0.0 copy-done
  285.4 2.1 convolution_convert_fusion.3
  287.5 21.9 %all_gather.17 = bf16[128,1024]{0,1:T(8,128)(2,1)S(1)} all-gather(bf16[128,64]{0,1:T(8,128)(2,1)S(1)} %convolution_convert_fusion.3), channel_id=1, replica_groups=mesh['dp'=32,'tensor'=16] {'tensor'}, dimensions={1}, use_global_device_ids=true | all-gather | bytes 278528 | tf_op jit(solution)/shard_map/all_gather | solution.py:78
  309.4 0.2 multiply_cosine_fusion
  309.6 0.1 copy.24
  309.7 0.1 copy.26
  309.8 122.8 %all-gather.8.cloned.1.call-done = bf16[8192,512]{1,0:T(8,128)(2,1)} async-done(((bf16[256,512]{1,0:T(8,128)(2,1)}), bf16[8192,512]{1,0:T(8,128)(2,1)}) %all-gather.8.cloned.1.call-update) | async-done | bytes 8388624 | tf_op jit(solution)/shard_map/all_gather | solution.py:69
  432.7 4.6 fusion.12
  437.3 0.1 reshape.74
  437.4 0.2 fusion.58
  437.6 0.1 subtract_convert_fusion.1
  437.7 0.3 fusion.27
  438.0 0.2 fusion.13
  438.2 0.2 fusion.8
  438.4 0.3 convolution_bitcast_fusion.3
  438.7 0.2 fusion.42
  439.0 0.2 fusion.14
  439.2 0.0 copy-start.3
  439.2 0.7 copy-done.3
  439.9 0.0 reduce-scatter.3.cloned.1.call-update
  440.0 0.0 reduce-scatter.5.cloned.1.call-start
  440.0 0.2 convolution_bitcast_fusion
  440.3 0.1 add_convert_fusion
  440.4 0.1 pad_maximum_fusion.1
  440.5 0.1 copy.34
  440.7 0.0 copy-start.1
  440.7 8.3 %fusion.59 = f32[128,8192]{1,0:T(8,128)} fusion(bf16[128,512]{0,1:T(8,128)(2,1)S(1)} %bitcast.91, bf16[8192,512]{1,0:T(8,128)(2,1)} %all-gather.8.cloned.1.call-done), kind=kOutput, calls=%fused_computation.88 | convolution fusion | flops 1073741824 | bytes 12713984 | tf_op jit(solution)/shard_map/dot_general | solution.py:130
  449.0 72.2 %reduce-scatter.3.cloned.1.call-done = bf16[128,64]{0,1:T(8,128)(2,1)} async-done(((bf16[128,1024]{0,1:T(8,128)(2,1)}), bf16[128,64]{0,1:T(8,128)(2,1)}) %reduce-scatter.3.cloned.1.call-update) | async-done | bytes 16400 | tf_op jit(solution)/shard_map/reduce_scatter | solution.py:127
  521.1 0.0 copy-done.1
  521.1 4.3 fusion.1
  525.4 0.0 copy-start.5
  525.4 0.0 reduce-scatter.5.cloned.1.call-update
  525.4 0.7 copy-done.5
  526.1 0.0 copy-start.2
  526.1 66.4 %all_gather.19 = bf16[4096,64]{0,1:T(8,128)(2,1)S(1)} all-gather(bf16[128,64]{0,1:T(8,128)(2,1)S(1)} %copy-done.5), channel_id=1, replica_groups=mesh['dp'=32,'tensor'=16] {'dp'}, dimensions={0}, use_global_device_ids=true | all-gather | bytes 540672 | tf_op jit(solution)/shard_map/all_gather | solution.py:154
  592.5 0.0 all-to-all-done
  592.5 2.7 convolution_convert_fusion.2
  595.2 24.5 %reduce-scatter.5.cloned.1.call-done = bf16[512,128]{0,1:T(8,128)(2,1)} async-done(((bf16[8192,128]{0,1:T(8,128)(2,1)}), bf16[512,128]{0,1:T(8,128)(2,1)}) %reduce-scatter.5.cloned.1.call-update) | async-done | bytes 131088 | tf_op jit(solution)/shard_map/reduce_scatter | solution.py:134
  619.7 0.0 copy-done.2
  619.7 1.1 fusion.24
  620.8 33.6 %psum.22 = f32[128,1]{0,1:T(1,128)S(1)} all-reduce(f32[128,1]{0,1:T(1,128)S(1)} %bitcast.93), channel_id=1, replica_groups=mesh['dp'=32,'tensor'=16] {'tensor'}, use_global_device_ids=true, to_apply=%region_7.8 | all-reduce | flops 128 | bytes 1024 | tf_op jit(solution)/shard_map/psum | solution.py:149
  654.4 65.2 %psum.23 = f32[512]{0:T(512)} all-reduce(f32[512]{0:T(512)S(1)} %get-tuple-element.3), channel_id=1, replica_groups=mesh['dp'=32,'tensor'=16] {'dp'}, use_global_device_ids=true, to_apply=%region_9.10 | all-reduce | flops 512 | bytes 4096 | tf_op jit(solution)/shard_map/psum | solution.py:153
  719.6 1.7 fusion.23
  (8 shorter events, 0.1 us)
Async XLA Ops:
  7.2 103.8 %all-gather.4.cloned.1.call-start = ((), (), s32[]{:S(2)}) async-start(), calls=%async_computation.3 | async-start | bytes 2228224 | tf_op jit(solution)/shard_map/all_gather | solution.py:67
  45.8 239.6 %all-gather.6.cloned.1.call-start = ((), (), s32[]{:S(2)}) async-start(), calls=%async_computation.4 | async-start | bytes 1081344 | tf_op jit(solution)/shard_map/all_gather | solution.py:70
  46.6 386.1 %all-gather.8.cloned.1.call-start = ((), (), s32[]{:S(2)}) async-start(), calls=%async_computation.5 | async-start | bytes 8650752 | tf_op jit(solution)/shard_map/all_gather | solution.py:69
  114.2 14.4 %copy-start.4 = (bf16[128,512]{1,0:T(8,128)(2,1)S(1)}, bf16[128,512]{1,0:T(8,128)(2,1)}, u32[]{:S(2)}) copy-start(bf16[128,512]{1,0:T(8,128)(2,1)} %param.6) | copy-start | bytes 393220
  114.2 171.2 %copy-start = (bf16[128,8192]{1,0:T(8,128)(2,1)S(1)}, bf16[128,8192]{1,0:T(8,128)(2,1)}, u32[]{:S(2)}) copy-start(bf16[128,8192]{1,0:T(8,128)(2,1)} %all-gather.4.cloned.1.call-done) | copy-start | bytes 6291460
  114.2 478.4 %all-to-all-start = ((bf16[128,32,256]{2,0,1:T(8,128)(2,1)}), bf16[128,32,256]{2,0,1:T(8,128)(2,1)}, u32[]{:S(2)}, u32[]{:S(2)}) async-start(bf16[128,32,256]{2,0,1:T(8,128)(2,1)} %bitcast.87), calls=%async_computation.2 | async-start | bytes 4194304 | tf_op jit(solution)/shard_map/all_to_all | solution.py:155
  128.5 392.6 %reduce-scatter.3.cloned.1.call-start = ((), (), s32[]{:S(2)}) async-start(), calls=%async_computation.6 | async-start | bytes 278528 | tf_op jit(solution)/shard_map/reduce_scatter | solution.py:127
  439.2 0.7 copy-start.3
  440.0 179.7 %reduce-scatter.5.cloned.1.call-start = ((), (), s32[]{:S(2)}) async-start(), calls=%async_computation.7 | async-start | bytes 2228224 | tf_op jit(solution)/shard_map/reduce_scatter | solution.py:134
  440.7 80.5 %copy-start.1 = (bf16[8192,64]{0,1:T(8,128)(2,1)S(1)}, bf16[8192,64]{0,1:T(8,128)(2,1)}, u32[]{:S(2)}) copy-start(bf16[8192,64]{0,1:T(8,128)(2,1)} %all-gather.6.cloned.1.call-done) | copy-start | bytes 3145732
  525.4 0.7 copy-start.5
  526.1 93.5 %copy-start.2 = (bf16[128,512]{1,0:T(8,128)(2,1)S(1)}, bf16[128,512]{1,0:T(8,128)(2,1)}, u32[]{:S(2)}) copy-start(bf16[128,512]{1,0:T(8,128)(2,1)} %param.5) | copy-start | bytes 393220
Sparse Core Ops, SparseCore 0:
  45.9 65.0 all-gather.3
  113.0 172.3 all-gather.5
  287.5 145.1 all-gather.7
  440.1 80.9 reduce-scatter.2
  526.5 93.0 reduce-scatter.4
where the time goes:
time: 728 us
  waiting for transfers between devices  441 us (61%)
  blocking collectives  222 us (30%)
  matrix products  23.4 us (3%)
  starting transfers between devices  14.6 us (2%)
  between operations  14 us (2%)
    all_gather x1, waiting for transfers between devices, on_device(): lax.all_gather(w_keyval, 'dp', axis=0, tiled=True)  157 us
    all_gather x1, waiting for transfers between devices, on_device(): lax.all_gather(w_query, 'dp', axis=0, tiled=True)  123 us
    reduce_scatter x1, waiting for transfers between devices, on_device(): lax.psum_scatter(grad_terms.astype(jnp.bfloat16), 'tensor', scatter_dimen...  72.2 us
    all_gather x1, blocking collectives, on_device(): keyval_all = lax.all_gather(grad_keyval, 'dp', axis=0, tiled=True)  66.4 us
    psum x1, blocking collectives, on_device(): grad_gain = lax.psum(jnp.sum(grad_normed * unit_rows, axis=0), 'dp')  65.2 us
    all_gather x1, waiting for transfers between devices, on_device(): normed_full = lax.all_gather(normed, 'tensor', axis=1, tiled=True)  63.7 us
    psum x1, blocking collectives, on_device(): lax.psum(jnp.sum(as_float * as_float, axis=1, keepdims=True), 'tensor')  35.1 us
    psum x1, blocking collectives, on_device(): lax.psum(jnp.sum(scaled_grad * unit_rows, axis=1, keepdims=True), 'tensor')  33.6 us
  transfers between devices with their start and end apart: 6, of which 5 were waited for; matrix products, arithmetic and copies ran while one was open for 4% of the time, Pallas kernels for 0%

commit v1 on v0

--- a/solution.py
+++ b/solution.py
@@ -64,7 +64,10 @@
     inv_rms = lax.rsqrt(row_sum / model_width + 1e-05)
     unit_rows = as_float * inv_rms
     normed = (unit_rows * gain_local).astype(jnp.bfloat16)
-    normed_full = lax.all_gather(normed, "tensor", axis=1, tiled=True)
+    count = lax.axis_size("tensor")
+    blocks = jnp.stack([normed for _ in range(count)])
+    blocks = lax.all_to_all(blocks, "tensor", split_axis=0, concat_axis=0)
+    normed_full = jnp.concatenate(blocks, axis=1)
     query_weight, keyweight = (
         lax.all_gather(w_query, "dp", axis=0, tiled=True),
         lax.all_gather(w_keyval, "dp", axis=0, tiled=True),

time: 728 us -> 633 us (0.87)
  waiting for transfers between devices: 441 us -> 298 us
  blocking collectives: 222 us -> 270 us
    all_gather x1, waiting for transfers between devices: 157 us -> 74.4 us  [on_device(): lax.all_gather(w_keyval, 'dp', axis=0, tiled=True)]
    all_gather x1 -> x0, waiting for transfers between devices: 63.7 us -> none  [on_device(): normed_full = lax.all_gather(normed, 'tensor', axis=1, tiled=True)]
    all_to_all x0 -> x1, blocking collectives: none -> 33.8 us  [on_device(): blocks = lax.all_to_all(blocks, 'tensor', split_axis=0, concat_axis=0)]
    all_gather x1, blocking collectives: 21.9 us -> 35.5 us  [on_device(): keyval_full = lax.all_gather(keyval_part, 'tensor', axis=1, tiled=True)]
  transfers between devices with their start and end apart: 6 -> 5, of which waited for: 5 -> 4; matrix products, arithmetic and copies ran while one was open for 4% -> 5% of each run, Pallas kernels for 0% -> 0%
where the time goes in v1:
time: 633 us
  waiting for transfers between devices  298 us (47%)
  blocking collectives  270 us (43%)
  matrix products  24.4 us (4%)
  starting transfers between devices  15.4 us (2%)
  between operations  14 us (2%)
    all_gather x1, waiting for transfers between devices, on_device(): lax.all_gather(w_query, 'dp', axis=0, tiled=True)  128 us
    all_gather x1, waiting for transfers between devices, on_device(): lax.all_gather(w_keyval, 'dp', axis=0, tiled=True)  74.4 us
    reduce_scatter x1, waiting for transfers between devices, on_device(): lax.psum_scatter(grad_terms.astype(jnp.bfloat16), 'tensor', scatter_dimen...  71.6 us
    all_gather x1, blocking collectives, on_device(): keyval_all = lax.all_gather(grad_keyval, 'dp', axis=0, tiled=True)  66.4 us
    psum x1, blocking collectives, on_device(): grad_gain = lax.psum(jnp.sum(grad_normed * unit_rows, axis=0), 'dp')  65.2 us
    all_gather x1, blocking collectives, on_device(): keyval_full = lax.all_gather(keyval_part, 'tensor', axis=1, tiled=True)  35.5 us
    psum x1, blocking collectives, on_device(): lax.psum(jnp.sum(as_float * as_float, axis=1, keepdims=True), 'tensor')  35.1 us
    all_to_all x1, blocking collectives, on_device(): blocks = lax.all_to_all(blocks, 'tensor', split_axis=0, concat_axis=0)  33.8 us
  transfers between devices with their start and end apart: 5, of which 4 were waited for; matrix products, arithmetic and copies ran while one was open for 5% of the time, Pallas kernels for 0%

profile of v1, /device:TPU:16, one launch (start us, length us, event | category | flops | bytes accessed | tf_op | source)
XLA Modules:
  0.0 633.0 jit_solution(2102129585782429171)
XLA Ops:
  7.2 0.0 all-gather.3.cloned.1.call-start
  7.2 0.7 all-gather.3.cloned.1.call-update
  7.9 0.0 all-gather.5.cloned.1.call-start
  7.9 0.7 all-gather.5.cloned.1.call-update
  8.7 0.8 dynamic_slice.9
  9.4 1.0 fusion.25
  10.4 35.1 %psum.21 = f32[128,1]{0,1:T(1,128)S(1)} all-reduce(f32[128,1]{0,1:T(1,128)S(1)} %bitcast.94), channel_id=1, replica_groups=mesh['dp'=32,'tensor'=16] {'tensor'}, use_global_device_ids=true, to_apply=%region_1.0 | all-reduce | flops 128 | bytes 1024 | tf_op jit(solution)/shard_map/psum | solution.py:63
  45.6 1.0 fusion.19
  46.6 0.1 copy.23
  46.7 0.4 stack.2
  47.1 33.8 %all_to_all.24 = bf16[16,128,512]{1,2,0:T(8,128)(2,1)} all-to-all(bf16[16,128,512]{1,2,0:T(8,128)(2,1)S(1)} %stack.2), channel_id=1, replica_groups=mesh['dp'=32,'tensor'=16] {'tensor'}, dimensions={0} | all-to-all | bytes 4194304 | tf_op jit(solution)/shard_map/all_to_all | solution.py:69
  80.9 0.0 copy-start.3
  80.9 15.3 %all-to-all-start.1 = ((bf16[128,32,256]{0,2,1:T(8,128)(2,1)}), bf16[128,32,256]{0,2,1:T(8,128)(2,1)S(1)}, u32[]{:S(2)}, u32[]{:S(2)}) async-start(bf16[128,32,256]{0,2,1:T(8,128)(2,1)} %bitcast.22), calls=%async_computation.3 | async-start | bytes 4194304 | tf_op jit(solution)/shard_map/all_to_all | solution.py:158
  96.2 0.0 reduce-scatter.3.cloned.1.call-start
  96.2 0.0 copy-done.3
  96.2 0.1 copy.29
  96.4 74.4 %all-gather.3.cloned.1.call-done = bf16[8192,64]{0,1:T(8,128)(2,1)} async-done(((bf16[256,64]{0,1:T(8,128)(2,1)}), bf16[8192,64]{0,1:T(8,128)(2,1)}) %all-gather.3.cloned.1.call-update) | async-done | bytes 1048592 | tf_op jit(solution)/shard_map/all_gather | solution.py:73
  170.9 2.4 convolution_convert_fusion.3
  173.3 35.5 %all_gather.13 = bf16[128,1024]{0,1:T(8,128)(2,1)S(1)} all-gather(bf16[128,64]{0,1:T(8,128)(2,1)S(1)} %convolution_convert_fusion.3), channel_id=1, replica_groups=mesh['dp'=32,'tensor'=16] {'tensor'}, dimensions={1}, use_global_device_ids=true | all-gather | bytes 278528 | tf_op jit(solution)/shard_map/all_gather | solution.py:81
  208.8 0.2 multiply_cosine_fusion
  209.0 0.1 copy.25
  209.1 0.1 copy.27
  209.2 128.4 %all-gather.5.cloned.1.call-done = bf16[8192,512]{1,0:T(8,128)(2,1)} async-done(((bf16[256,512]{1,0:T(8,128)(2,1)}), bf16[8192,512]{1,0:T(8,128)(2,1)}) %all-gather.5.cloned.1.call-update) | async-done | bytes 8388624 | tf_op jit(solution)/shard_map/all_gather | solution.py:72
  337.6 5.3 fusion.12
  342.9 0.1 reshape.85
  343.0 0.2 fusion.58
  343.2 0.1 subtract_convert_fusion.1
  343.3 0.3 fusion.27
  343.6 0.2 fusion.13
  343.8 0.2 fusion.8
  344.1 0.3 convolution_bitcast_fusion.3
  344.4 0.2 fusion.42
  344.7 0.2 fusion.14
  344.9 0.0 copy-start.2
  344.9 0.7 copy-done.2
  345.6 0.0 reduce-scatter.3.cloned.1.call-update
  345.6 0.0 reduce-scatter.5.cloned.1.call-start
  345.6 0.2 convolution_bitcast_fusion
  345.9 0.1 add_convert_fusion
  346.0 0.1 pad_maximum_fusion.1
  346.2 0.1 copy.35
  346.3 0.0 copy-start
  346.3 8.3 %fusion.59 = f32[128,8192]{1,0:T(8,128)} fusion(bf16[128,512]{0,1:T(8,128)(2,1)S(1)} %bitcast.91, bf16[8192,512]{1,0:T(8,128)(2,1)} %all-gather.5.cloned.1.call-done), kind=kOutput, calls=%fused_computation.87 | convolution fusion | flops 1073741824 | bytes 12713984 | tf_op jit(solution)/shard_map/dot_general | solution.py:133
  354.6 71.6 %reduce-scatter.3.cloned.1.call-done = bf16[128,64]{0,1:T(8,128)(2,1)} async-done(((bf16[128,1024]{0,1:T(8,128)(2,1)}), bf16[128,64]{0,1:T(8,128)(2,1)}) %reduce-scatter.3.cloned.1.call-update) | async-done | bytes 16400 | tf_op jit(solution)/shard_map/reduce_scatter | solution.py:130
  426.2 0.0 copy-done
  426.2 4.3 fusion.1
  430.5 0.0 reduce-scatter.5.cloned.1.call-update
  430.5 0.0 all-to-all-done.1
  430.5 0.0 copy-start.4
  430.5 2.9 copy.40
  433.5 0.0 copy-done.4
  433.5 0.0 copy-start.1
  433.5 66.4 %all_gather.15 = bf16[4096,64]{0,1:T(8,128)(2,1)S(1)} all-gather(bf16[128,64]{0,1:T(8,128)(2,1)S(1)} %copy-done.4), channel_id=1, replica_groups=mesh['dp'=32,'tensor'=16] {'dp'}, dimensions={0}, use_global_device_ids=true | all-gather | bytes 540672 | tf_op jit(solution)/shard_map/all_gather | solution.py:157
  499.8 2.7 convolution_convert_fusion.2
  502.5 22.3 %reduce-scatter.5.cloned.1.call-done = bf16[512,128]{0,1:T(8,128)(2,1)} async-done(((bf16[8192,128]{0,1:T(8,128)(2,1)}), bf16[512,128]{0,1:T(8,128)(2,1)}) %reduce-scatter.5.cloned.1.call-update) | async-done | bytes 131088 | tf_op jit(solution)/shard_map/reduce_scatter | solution.py:137
  524.8 0.0 copy-done.1
  524.8 1.1 fusion.24
  525.9 33.6 %psum.22 = f32[128,1]{0,1:T(1,128)S(1)} all-reduce(f32[128,1]{0,1:T(1,128)S(1)} %bitcast.93), channel_id=1, replica_groups=mesh['dp'=32,'tensor'=16] {'tensor'}, use_global_device_ids=true, to_apply=%region_7.8 | all-reduce | flops 128 | bytes 1024 | tf_op jit(solution)/shard_map/psum | solution.py:152
  559.6 65.2 %psum.23 = f32[512]{0:T(512)} all-reduce(f32[512]{0:T(512)S(1)} %get-tuple-element.3), channel_id=1, replica_groups=mesh['dp'=32,'tensor'=16] {'dp'}, use_global_device_ids=true, to_apply=%region_9.10 | all-reduce | flops 512 | bytes 4096 | tf_op jit(solution)/shard_map/psum | solution.py:156
  624.8 1.7 fusion.23
  (8 shorter events, 0.1 us)
Async XLA Ops:
  7.2 163.7 %all-gather.3.cloned.1.call-start = ((), (), s32[]{:S(2)}) async-start(), calls=%async_computation.4 | async-start | bytes 1081344 | tf_op jit(solution)/shard_map/all_gather | solution.py:73
  7.9 329.7 %all-gather.5.cloned.1.call-start = ((), (), s32[]{:S(2)}) async-start(), calls=%async_computation.5 | async-start | bytes 8650752 | tf_op jit(solution)/shard_map/all_gather | solution.py:72
  80.9 15.4 %copy-start.3 = (bf16[128,512]{1,0:T(8,128)(2,1)S(1)}, bf16[128,512]{1,0:T(8,128)(2,1)}, u32[]{:S(2)}) copy-start(bf16[128,512]{1,0:T(8,128)(2,1)} %param.6) | copy-start | bytes 393220
  80.9 349.6 %all-to-all-start.1 = ((bf16[128,32,256]{0,2,1:T(8,128)(2,1)}), bf16[128,32,256]{0,2,1:T(8,128)(2,1)S(1)}, u32[]{:S(2)}, u32[]{:S(2)}) async-start(bf16[128,32,256]{0,2,1:T(8,128)(2,1)} %bitcast.22), calls=%async_computation.3 | async-start | bytes 4194304 | tf_op jit(solution)/shard_map/all_to_all | solution.py:158
  96.2 330.0 %reduce-scatter.3.cloned.1.call-start = ((), (), s32[]{:S(2)}) async-start(), calls=%async_computation.6 | async-start | bytes 278528 | tf_op jit(solution)/shard_map/reduce_scatter | solution.py:130
  344.9 0.7 copy-start.2
  345.6 179.2 %reduce-scatter.5.cloned.1.call-start = ((), (), s32[]{:S(2)}) async-start(), calls=%async_computation.7 | async-start | bytes 2228224 | tf_op jit(solution)/shard_map/reduce_scatter | solution.py:137
  346.3 79.9 %copy-start = (bf16[8192,64]{0,1:T(8,128)(2,1)S(1)}, bf16[8192,64]{0,1:T(8,128)(2,1)}, u32[]{:S(2)}) copy-start(bf16[8192,64]{0,1:T(8,128)(2,1)} %all-gather.3.cloned.1.call-done) | copy-start | bytes 3145732
  430.5 2.9 copy-start.4
  433.5 91.4 %copy-start.1 = (bf16[128,512]{1,0:T(8,128)(2,1)S(1)}, bf16[128,512]{1,0:T(8,128)(2,1)}, u32[]{:S(2)}) copy-start(bf16[128,512]{1,0:T(8,128)(2,1)} %param.5) | copy-start | bytes 393220
Sparse Core Ops, SparseCore 0:
  10.0 160.8 all-gather.2
  172.9 164.6 all-gather.4
  345.7 80.4 reduce-scatter.2
  431.6 93.1 reduce-scatter.4
